TPU v7x, 32 devices: a whole 2x2x4 slice. The times are simulated.
32 devices in a mesh: row: 4 (over z), col: 8 (over y, x, core).
Axes of the slice: x: 2, y: 2, z: 4, core: 2. Of those that a mesh axis runs over, the one named last changes fastest.
Arguments:
- tokens: bfloat16 [2, 96, 128, 512], P(None, 'row', 'col'), may hold values from -6 to 6
- w_qkv: bfloat16 [512, 1536], replicated, may hold values from -0.25 to 0.25
- w_out: bfloat16 [512, 512], replicated, may hold values from -0.25 to 0.25
- q_saved: bfloat16 [2, 96, 128, 512], P(None, 'row', 'col'), may hold values from -4 to 4
- k_saved: bfloat16 [2, 96, 128, 512], P(None, 'row', 'col'), may hold values from -4 to 4
- v_saved: bfloat16 [2, 96, 128, 512], P(None, 'row', 'col'), may hold values from -4 to 4
- scale_exp: int32 [2, 12, 16, 24], P(None, 'row', 'col'), may hold values from -1 to 1
- grad_out: bfloat16 [2, 96, 128, 512], P(None, 'row', 'col'), may hold values from -6 to 6
- crop_start: int32 [2, 2], replicated, may hold values from 0 to 3
Outputs:
- grad_tokens: bfloat16 [2, 96, 128, 512], P(None, 'row', 'col')
- grad_w_qkv: float32 [512, 1536], P('row', 'col')
- grad_w_out: float32 [512, 512], P('row', 'col')
Inputs may be any that keep to these rules, and one draw needn't show every extreme that they name: crop_start[b] holds the first row and the first column of the region of frame b that the loss covers.
All inputs are finite; a program needn't handle non-finite values.
Results may differ from a plain program's by a relative error of at most 0.017.
Values may be sent and summed in bfloat16 or wider, within the bound.
A program may use at most 128 MiB of HBM per device.

v0:
```python
import math
import jax
import jax.numpy as jnp
from jax import lax
from jax.sharding import PartitionSpec as P

HEADS = 8
RADIUS = 4
BLOCK = 8
max_norm = 1000.0
masked_score = -1e30
tiny_square = 1e-06


def passed_along(array, axis, by):
    size = lax.axis_size(axis)
    pairs = [(i, i + by) for i in range(size) if 0 <= i + by < size]
    return lax.ppermute(array, axis, pairs)


def padded_2(cells, sides, width):
    for axis, dim in sides:
        count = lax.axis_size(axis)
        ends = count - 1
        head = lax.slice_in_dim(cells, 0, width, axis=dim)
        tail = lax.slice_in_dim(cells, cells.shape[dim] - width, cells.shape[dim], axis=dim)
        cells = jnp.concatenate(
            [
                lax.ppermute(tail, axis, [(i, (i + 1) % count) for i in range(ends)]),
                cells,
                lax.ppermute(head, axis, [((i + 1) % count, i) for i in range(ends)]),
            ],
            axis=dim,
        )
    return cells


def product(form, left, right):
    return jnp.einsum(form, left, right, preferred_element_type=jnp.float32)


def dequantize(mantissa, exponent):
    members, height, breadth, features = mantissa.shape
    heads = exponent.shape[3]
    factor = jnp.exp2(exponent.astype(jnp.float32))
    factor = jnp.repeat(jnp.repeat(factor, BLOCK, axis=1), BLOCK, axis=2)
    scaled = (
        mantissa.astype(jnp.float32).reshape(members, height, breadth, heads, features // heads)
        * factor[..., None]
    )
    return scaled.reshape(members, height, breadth, features).astype(jnp.bfloat16)


def query_tiles(tensor):
    height, breadth, features = tensor.shape
    blocked = tensor.reshape(
        height // BLOCK, BLOCK, breadth // BLOCK, BLOCK, HEADS, features // HEADS
    )
    return blocked.transpose(0, 2, 1, 3, 4, 5).reshape(
        height // BLOCK, breadth // BLOCK, BLOCK * BLOCK, HEADS, features // HEADS
    )


def query_untile(tile_set, height, breadth):
    tile_rows, tile_cols = (tile_set.shape[0], tile_set.shape[1])
    features = tile_set.shape[3] * tile_set.shape[4]
    blocked = tile_set.reshape(tile_rows, tile_cols, BLOCK, BLOCK, features)
    return blocked.transpose(0, 2, 1, 3, 4).reshape(height, breadth, features)


def key_tiles(padded):
    height, breadth, features = padded.shape
    tile_rows = height // BLOCK - 1
    tile_cols = breadth // BLOCK - 1
    blocked = padded.reshape(tile_rows + 1, BLOCK, tile_cols + 1, BLOCK, features)
    paired = jnp.stack([blocked[:-1], blocked[1:]], axis=1).reshape(
        tile_rows, 2 * BLOCK, tile_cols + 1, BLOCK, features
    )
    paired = jnp.stack([paired[:, :, :-1], paired[:, :, 1:]], axis=3).reshape(
        tile_rows, 2 * BLOCK, tile_cols, 2 * BLOCK, features
    )
    return paired.transpose(0, 2, 1, 3, 4).reshape(
        tile_rows, tile_cols, 4 * BLOCK * BLOCK, HEADS, features // HEADS
    )


def fold_keys(tile_set):
    tile_rows, tile_cols = (tile_set.shape[0], tile_set.shape[1])
    features = tile_set.shape[3] * tile_set.shape[4]
    tile_grid = tile_set.reshape(tile_rows, tile_cols, 2, BLOCK, 2, BLOCK, features).transpose(
        0, 2, 3, 1, 4, 5, 6
    )
    zero_row = jnp.zeros((1, BLOCK, tile_cols, 2, BLOCK, features), tile_set.dtype)
    summed = jnp.concatenate([tile_grid[:, 0], zero_row], 0) + jnp.concatenate(
        [zero_row, tile_grid[:, 1]], 0
    )
    zero_col = jnp.zeros((tile_rows + 1, BLOCK, 1, BLOCK, features), tile_set.dtype)
    summed = jnp.concatenate([summed[:, :, :, 0], zero_col], 2) + jnp.concatenate(
        [zero_col, summed[:, :, :, 1]], 2
    )
    return summed.reshape((tile_rows + 1) * BLOCK, (tile_cols + 1) * BLOCK, features)


def key_valid(anchor, tile_count, extent):
    position = (
        anchor
        + BLOCK * jnp.arange(tile_count, dtype=jnp.int32)[:, None]
        + jnp.arange(2 * BLOCK, dtype=jnp.int32)[None, :]
    )
    return (position >= 0) & (position < extent)


def window_mask():
    reach = (
        jnp.arange(2 * BLOCK, dtype=jnp.int32)[None, :]
        - jnp.arange(BLOCK, dtype=jnp.int32)[:, None]
    )
    inside = (reach >= 0) & (reach <= 2 * RADIUS)
    return (inside[:, None, :, None] & inside[None, :, None, :]).reshape(
        BLOCK * BLOCK, 4 * BLOCK * BLOCK
    )


def attend(
    queries, grads_attn, keys_pad, values_pad, row_anchor, col_anchor, frame_rows, frame_cols
):
    height, breadth, features = queries.shape
    score_scale = 1.0 / math.sqrt(features // HEADS)
    q_tiles = query_tiles(queries)
    g_tiles = query_tiles(grads_attn)
    k_tiles = key_tiles(keys_pad)
    v_tiles = key_tiles(values_pad)
    tile_rows, tile_cols = (q_tiles.shape[0], q_tiles.shape[1])
    row_ok = key_valid(row_anchor, tile_rows, frame_rows)
    col_ok = key_valid(col_anchor, tile_cols, frame_cols)
    keys_ok = (row_ok[:, None, :, None] & col_ok[None, :, None, :]).reshape(
        tile_rows, tile_cols, 1, 1, 4 * BLOCK * BLOCK
    )
    allowed = keys_ok & window_mask()[None, None, None]
    scores = product("ijqhd,ijkhd->ijhqk", q_tiles, k_tiles) * score_scale
    scores = jnp.where(allowed, scores, masked_score)
    row_max = jnp.max(scores, axis=-1, keepdims=True)
    weights = jnp.exp(scores - row_max)
    softmax = weights / jnp.sum(weights, axis=-1, keepdims=True)
    softmax_half = softmax.astype(jnp.bfloat16)
    out_tiles = product("ijhqk,ijkhd->ijqhd", softmax_half, v_tiles).astype(jnp.bfloat16)
    row_delta = product("ijqhd,ijqhd->ijhq", g_tiles, out_tiles)
    grad_probs = product("ijqhd,ijkhd->ijhqk", g_tiles, v_tiles)
    grad_scores = (softmax * (grad_probs - row_delta[..., None]) * score_scale).astype(jnp.bfloat16)
    grad_q_tiles = product("ijhqk,ijkhd->ijqhd", grad_scores, k_tiles)
    grad_k_tiles = product("ijhqk,ijqhd->ijkhd", grad_scores, q_tiles)
    grad_v_tiles = product("ijhqk,ijqhd->ijkhd", softmax_half, g_tiles)
    return (
        query_untile(out_tiles, height, breadth),
        query_untile(grad_q_tiles, height, breadth),
        fold_keys(grad_k_tiles),
        fold_keys(grad_v_tiles),
    )


def return_rims(padded_grads):
    interior = padded_grads[:, :, :, RADIUS:-RADIUS]
    for offset in (1, -1):
        border_part = (
            padded_grads[:, :, :, -RADIUS:] if offset == 1 else padded_grads[:, :, :, :RADIUS]
        )
        arrived = passed_along(border_part, "col", offset)
        if offset == 1:
            interior = interior.at[:, :, :, :RADIUS].add(arrived)
        else:
            interior = interior.at[:, :, :, -RADIUS:].add(arrived)
    owned = interior[:, :, RADIUS:-RADIUS]
    for offset in (1, -1):
        border_part = interior[:, :, -RADIUS:] if offset == 1 else interior[:, :, :RADIUS]
        arrived = passed_along(border_part, "row", offset)
        if offset == 1:
            owned = owned.at[:, :, :RADIUS].add(arrived)
        else:
            owned = owned.at[:, :, -RADIUS:].add(arrived)
    return owned


def body(tokens, w_qkv, w_out, q_saved, k_saved, v_saved, scale_exp, grad_out, crop_start):
    members, height, breadth, features = tokens.shape
    queries = dequantize(q_saved, scale_exp[..., :HEADS])
    keys_full = dequantize(k_saved, scale_exp[..., HEADS : 2 * HEADS])
    values = dequantize(v_saved, scale_exp[..., 2 * HEADS :])
    row_index = lax.axis_index("row")
    col_index = lax.axis_index("col")
    frame_rows = height * lax.axis_size("row")
    frame_cols = breadth * lax.axis_size("col")
    row_place = row_index * height + jnp.arange(height, dtype=jnp.int32)
    col_place = col_index * breadth + jnp.arange(breadth, dtype=jnp.int32)
    inside = (row_place[None, :, None] >= crop_start[:, 0][:, None, None]) & (
        col_place[None, None, :] >= crop_start[:, 1][:, None, None]
    )
    masked = jnp.where(inside[..., None], grad_out, jnp.zeros_like(grad_out))
    flat_grad = masked.reshape(-1, features)
    grad_attn = lax.dot_general(
        flat_grad, w_out, (((1,), (1,)), ((), ())), preferred_element_type=jnp.float32
    )
    grad_attn = grad_attn.astype(jnp.bfloat16).reshape(masked.shape)
    stacked = jnp.stack([keys_full, values])
    padded = padded_2(stacked, (("row", 2), ("col", 3)), RADIUS)

    def one_member(member):
        q_member, g_member, k_member, v_member = member
        return attend(
            q_member,
            g_member,
            k_member,
            v_member,
            row_index * height - RADIUS,
            col_index * breadth - RADIUS,
            frame_rows,
            frame_cols,
        )

    attn_out, grad_query, grad_k_pad, grad_v_pad = lax.map(
        one_member, (queries, grad_attn, padded[0], padded[1])
    )
    owned = return_rims(jnp.stack([grad_k_pad, grad_v_pad]))
    grad_key, grad_value = (owned[0], owned[1])
    flat_qkv = (
        jnp.concatenate([grad_query, grad_key, grad_value], axis=-1)
        .astype(jnp.bfloat16)
        .reshape(-1, 3 * features)
    )
    grad_tokens = lax.dot_general(
        flat_qkv, w_qkv, (((1,), (1,)), ((), ())), preferred_element_type=jnp.float32
    )
    grad_tokens = grad_tokens.astype(jnp.bfloat16).reshape(tokens.shape)
    raw_qkv = lax.dot_general(
        tokens.reshape(-1, features),
        flat_qkv,
        (((0,), (0,)), ((), ())),
        preferred_element_type=jnp.float32,
    )
    raw_out = lax.dot_general(
        attn_out.reshape(-1, features),
        flat_grad,
        (((0,), (0,)), ((), ())),
        preferred_element_type=jnp.float32,
    )
    whole_qkv, whole_out = lax.psum((raw_qkv, raw_out), ("row", "col"))
    squares = jnp.sum(whole_qkv * whole_qkv) + jnp.sum(whole_out * whole_out)
    rows_each = features // lax.axis_size("row")
    qkv_cols = 3 * features // lax.axis_size("col")
    out_cols = features // lax.axis_size("col")
    part_qkv = lax.dynamic_slice(
        whole_qkv, (row_index * rows_each, col_index * qkv_cols), (rows_each, qkv_cols)
    )
    part_out = lax.dynamic_slice(
        whole_out, (row_index * rows_each, col_index * out_cols), (rows_each, out_cols)
    )
    factor = jnp.minimum(1.0, max_norm / jnp.sqrt(squares + tiny_square))
    return (grad_tokens, factor * part_qkv, factor * part_out)


def solution(mesh):
    placed = (
        P(None, "row", "col", None),
        P(),
        P(),
        P(None, "row", "col", None),
        P(None, "row", "col", None),
        P(None, "row", "col", None),
        P(None, "row", "col", None),
        P(None, "row", "col", None),
        P(),
    )
    return jax.shard_map(
        body,
        mesh=mesh,
        in_specs=placed,
        out_specs=(P(None, "row", "col", None), P("row", "col"), P("row", "col")),
        check_vma=False,
    )
```

profile of v0, /device:TPU:0, one launch (start us, length us, event | category | flops | bytes accessed | tf_op | source)
XLA Modules:
  0.0 465.0 jit_solution(9168266061171627752)
XLA Ops:
  8.2 2.1 mul.120
  10.3 3.8 mul.121
  14.1 2.1 mul.124
  16.3 3.7 mul.125
  20.0 2.9 fusion.51
  25.1 6.3 %collective-permute-start = (bf16[2,2,4,16,512]{4,3,2,1,0:T(8,128)(2,1)}, bf16[2,2,4,16,512]{4,3,2,1,0:T(8,128)(2,1)}, u32[]{:S(2)}, u32[]{:S(2)}) collective-permute-start(bf16[2,2,4,16,512]{4,3,2,1,0:T(8,128)(2,1)} %get-tuple-element.293), channel_id=1, source_target_pairs={{0,8},{8,16},{16,24},{1,9},{9,17},{17,25},{2,10},{10,18},{18,26},{... | collective-permute-start | bytes 786440 | tf_op jit(solution)/shard_map/ppermute | solution.py:29
  31.5 2.1 mul.130
  33.6 3.8 mul.131
  42.3 3.1 collective-permute-start.2
  48.1 3.2 pad_maximum_fusion.4
  51.3 1.9 slice_bitcast_fusion.8
  53.1 190.3 %while.24 = (s32[]{:T(128)}, bf16[2,24,16,512]{3,2,1,0:T(8,128)(2,1)}, bf16[2,24,16,512]{3,1,2,0:T(8,128)(2,1)}, f32[2,32,24,512]{3,1,2,0:T(8,128)}, f32[2,32,24...) while((s32[]{:T(128)}, ...), condition=%wide.region_3.4_spmd.clone, body=%wide.region_0.3_spmd.sunk.clone | while | flops 621461056 | bytes 255329296 | solution.py:219
  56.8 1.7 copy.192
  60.5 3.0 reshape.547
  63.5 4.5 copy.194
  68.8 3.0 reshape.548
  71.7 3.4 copy.196
  77.5 3.3 fusion.117
  81.8 4.4 fusion.120
  86.2 2.5 multiply_reduce_fusion.5
  88.8 2.4 copy.197
  91.2 1.7 reshape.550
  93.8 3.5 multiply_convert_fusion.6
  103.0 4.4 convolution_bitcast_fusion.12
  107.4 5.9 %copy.201 = f32[3,2,256,8,64]{4,3,2,1,0:T(8,128)} copy(f32[3,2,256,8,64]{2,4,3,1,0:T(8,128)} %convolution_bitcast_fusion.12) | data formatting | bytes 6291456 | tf_op jit(solution)/shard_map/while/body/eval_jaxpr/ijhqk,ijqhd->ijkhd/transpose | solution.py:39
  113.3 6.2 %reshape.552 = f32[3,2,2,8,2,8,512]{6,5,4,3,2,1,0:T(8,128)} reshape(f32[3,2,256,8,64]{4,3,2,1,0:T(8,128)} %copy.201) | data formatting | bytes 6291456 | tf_op jit(solution)/shard_map/while/body/eval_jaxpr/reshape | solution.py:90
  119.5 2.2 slice_bitcast_fusion.20
  123.7 2.3 convolution_bitcast_fusion.13
  126.0 5.9 %copy.203 = f32[3,2,256,8,64]{4,3,2,1,0:T(8,128)} copy(f32[3,2,256,8,64]{2,4,3,1,0:T(8,128)} %convolution_bitcast_fusion.13) | data formatting | bytes 6291456 | tf_op jit(solution)/shard_map/while/body/eval_jaxpr/ijhqk,ijqhd->ijkhd/transpose | solution.py:39
  131.8 6.2 %reshape.553 = f32[3,2,2,8,2,8,512]{6,5,4,3,2,1,0:T(8,128)} reshape(f32[3,2,256,8,64]{4,3,2,1,0:T(8,128)} %copy.203) | data formatting | bytes 6291456 | tf_op jit(solution)/shard_map/while/body/eval_jaxpr/reshape | solution.py:90
  138.1 2.2 slice_bitcast_fusion.21
  143.5 2.1 copy_dynamic-update-slice_fusion.8
  145.7 1.7 copy-done.9
  151.9 1.7 copy.192
  155.6 3.0 reshape.547
  158.6 4.5 copy.194
  163.9 3.0 reshape.548
  166.9 3.4 copy.196
  172.7 3.3 fusion.117
  177.0 4.4 fusion.120
  181.4 2.5 multiply_reduce_fusion.5
  183.9 2.4 copy.197
  186.3 1.7 reshape.550
  188.9 3.5 multiply_convert_fusion.6
  198.1 4.4 convolution_bitcast_fusion.12
  202.6 5.9 %copy.201 = f32[3,2,256,8,64]{4,3,2,1,0:T(8,128)} copy(f32[3,2,256,8,64]{2,4,3,1,0:T(8,128)} %convolution_bitcast_fusion.12) | data formatting | bytes 6291456 | tf_op jit(solution)/shard_map/while/body/eval_jaxpr/ijhqk,ijqhd->ijkhd/transpose | solution.py:39
  208.5 6.2 %reshape.552 = f32[3,2,2,8,2,8,512]{6,5,4,3,2,1,0:T(8,128)} reshape(f32[3,2,256,8,64]{4,3,2,1,0:T(8,128)} %copy.201) | data formatting | bytes 6291456 | tf_op jit(solution)/shard_map/while/body/eval_jaxpr/reshape | solution.py:90
  214.7 2.2 slice_bitcast_fusion.20
  218.9 2.3 convolution_bitcast_fusion.13
  221.2 5.9 %copy.203 = f32[3,2,256,8,64]{4,3,2,1,0:T(8,128)} copy(f32[3,2,256,8,64]{2,4,3,1,0:T(8,128)} %convolution_bitcast_fusion.13) | data formatting | bytes 6291456 | tf_op jit(solution)/shard_map/while/body/eval_jaxpr/ijhqk,ijqhd->ijkhd/transpose | solution.py:39
  227.0 6.2 %reshape.553 = f32[3,2,2,8,2,8,512]{6,5,4,3,2,1,0:T(8,128)} reshape(f32[3,2,256,8,64]{4,3,2,1,0:T(8,128)} %copy.203) | data formatting | bytes 6291456 | tf_op jit(solution)/shard_map/while/body/eval_jaxpr/reshape | solution.py:90
  233.3 2.2 slice_bitcast_fusion.21
  238.7 2.1 copy_dynamic-update-slice_fusion.8
  240.8 1.7 copy-done.9
  244.9 8.3 %collective-permute-start.4 = (f32[2,2,32,4,512]{4,2,3,1,0:T(8,128)S(1)}, f32[2,2,32,4,512]{4,2,3,1,0:T(8,128)S(1)}, u32[]{:S(2)}, u32[]{:S(2)}) collective-permute-start(f32[2,2,32,4,512]{4,2,3,1,0:T(8,128)S(1)} %fusion.46), channel_id=1, source_target_pairs={{0,1},{1,2},{2,3},{3,4},{4,5},{5,6},{6,7},{8,9},{9,10},{10,11},{11... | collective-permute-start | bytes 3145736 | tf_op jit(solution)/shard_map/ppermute | solution.py:18
  257.2 13.4 %collective-permute-done.5 = f32[2,2,32,4,512]{4,2,3,1,0:T(8,128)S(1)} collective-permute-done((f32[2,2,32,4,512]{4,2,3,1,0:T(8,128)S(1)}, f32[2,2,32,4,512]{4,2,3,1,0:T(8,128)S(1)}, u32[]{:S(2)}, u32[]{:S(2)}) %collective-permute-start.5) | collective-permute-done | bytes 1048608 | tf_op jit(solution)/shard_map/ppermute | solution.py:18
  271.2 2.8 collective-permute-start.6
  275.3 1.7 convolution_bitcast_fusion.4
  277.6 3.1 collective-permute-done.6
  281.0 4.1 collective-permute-done.7
  285.6 3.2 convolution_bitcast_fusion.3
  290.7 2.3 fusion.43
  293.0 157.2 %all-reduce.11.cloned.1.call-done = (f32[512,1536]{0,1:T(8,128)}, f32[512,512]{1,0:T(8,128)}) async-done(((f32[512,1536]{0,1:T(8,128)}, f32[512,512]{1,0:T(8,128)}), (f32[512,1536]{0,1:T(8,128)}, f32[512,512]{1,0:T(8,128)})) %all-reduce.11.cloned.1.call-update) | async-done | bytes 4194320 | tf_op jit(solution)/shard_map/psum | solution.py:245
  450.2 3.4 multiply_reduce_fusion.1
  (207 shorter events, 68.7 us)
Async XLA Ops:
  7.2 283.5 %copy-start = (bf16[512,1536]{1,0:T(8,128)(2,1)S(1)}, bf16[512,1536]{1,0:T(8,128)(2,1)}, u32[]{:S(2)}) copy-start(bf16[512,1536]{1,0:T(8,128)(2,1)} %param.20) | copy-start | bytes 4718596
  7.2 443.0 %all-reduce.11.cloned.1.call-start = ((), (), s32[]{:S(2)}) async-start(), calls=%async_computation | async-start | bytes 8388608 | tf_op jit(solution)/shard_map/psum | solution.py:245
  23.8 15.5 %collective-permute-start.1 = (bf16[2,2,4,16,512]{4,3,2,1,0:T(8,128)(2,1)}, bf16[2,2,4,16,512]{4,3,2,1,0:T(8,128)(2,1)S(1)}, u32[]{:S(2)}, u32[]{:S(2)}) collective-permute-start(bf16[2,2,4,16,512]{4,3,2,1,0:T(8,128)(2,1)} %get-tuple-element.294), channel_id=1, source_target_pairs={{8,0},{16,8},{24,16},{9,1},{17,9},{25,17},{10,2},{18,10},{26,18},{... | collective-permute-start | bytes 786440 | tf_op jit(solution)/shard_map/ppermute | solution.py:31
  25.1 14.2 %collective-permute-start = (bf16[2,2,4,16,512]{4,3,2,1,0:T(8,128)(2,1)}, bf16[2,2,4,16,512]{4,3,2,1,0:T(8,128)(2,1)}, u32[]{:S(2)}, u32[]{:S(2)}) collective-permute-start(bf16[2,2,4,16,512]{4,3,2,1,0:T(8,128)(2,1)} %get-tuple-element.293), channel_id=1, source_target_pairs={{0,8},{8,16},{16,24},{1,9},{9,17},{17,25},{2,10},{10,18},{18,26},{... | collective-permute-start | bytes 786440 | tf_op jit(solution)/shard_map/ppermute | solution.py:29
  33.6 3.8 copy-start.20
  37.4 7.9 %copy-start.23 = (bf16[512,512]{1,0:T(8,128)(2,1)S(1)}, bf16[512,512]{1,0:T(8,128)(2,1)}, u32[]{:S(2)}) copy-start(bf16[512,512]{1,0:T(8,128)(2,1)} %param.21) | copy-start | bytes 1572868
  37.8 9.1 %copy-start.14 = (f32[2,24,16,512]{3,2,1,0:T(8,128)S(1)}, f32[2,24,16,512]{3,2,1,0:T(8,128)}, u32[]{:S(2)}) copy-start(f32[2,24,16,512]{3,2,1,0:T(8,128)} %mul.131) | copy-start | bytes 4718596
  37.8 9.1 %copy-start.19 = (bf16[2,24,16,512]{3,2,1,0:T(8,128)(2,1)S(1)}, bf16[2,24,16,512]{3,2,1,0:T(8,128)(2,1)}, u32[]{:S(2)}) copy-start(bf16[2,24,16,512]{3,2,1,0:T(8,128)(2,1)} %param.22) | copy-start | bytes 2359300
  39.3 8.8 %copy-start.16 = (bf16[2,24,16,512]{3,2,1,0:T(8,128)(2,1)}, bf16[2,24,16,512]{3,2,1,0:T(8,128)(2,1)S(1)}, u32[]{:S(2)}) copy-start(bf16[2,24,16,512]{3,2,1,0:T(8,128)(2,1)S(1)} %broadcast_select_fusion) | copy-start | bytes 2359300
  41.0 7.1 %collective-permute-start.3 = (bf16[2,2,32,4,512]{4,3,2,1,0:T(4,128)(2,1)S(1)}, bf16[2,2,32,4,512]{4,3,2,1,0:T(4,128)(2,1)S(1)}, u32[]{:S(2)}, u32[]{:S(2)}) collective-permute-start(bf16[2,2,32,4,512]{4,3,2,1,0:T(4,128)(2,1)S(1)} %get-tuple-element.292), channel_id=1, source_target_pairs={{1,0},{2,1},{3,2},{4,3},{5,4},{6,5},{7,6},{9,8},{10,9},{11,10},{12... | collective-permute-start | bytes 1572872 | tf_op jit(solution)/shard_map/ppermute | solution.py:31
  42.3 5.8 %collective-permute-start.2 = (bf16[2,2,32,4,512]{4,3,2,1,0:T(4,128)(2,1)S(1)}, bf16[2,2,32,4,512]{4,3,2,1,0:T(4,128)(2,1)S(1)}, u32[]{:S(2)}, u32[]{:S(2)}) collective-permute-start(bf16[2,2,32,4,512]{4,3,2,1,0:T(4,128)(2,1)S(1)} %get-tuple-element.291), channel_id=1, source_target_pairs={{0,1},{1,2},{2,3},{3,4},{4,5},{5,6},{6,7},{8,9},{9,10},{10,11},{11... | collective-permute-start | bytes 1572872 | tf_op jit(solution)/shard_map/ppermute | solution.py:29
  63.5 4.5 copy-start.7
  81.8 4.4 copy-start.5
  81.8 4.4 copy-start.6
  86.2 2.6 copy-start.24
  86.2 2.6 copy-start.25
  97.3 1.1 copy-start.1
  99.8 3.1 copy-start.4
  122.1 1.4 copy-start.2
  122.1 1.6 copy-start.3
  140.7 1.9 copy-start.8
  140.7 2.8 copy-start.11
  145.6 1.7 copy-start.9
  145.7 2.6 copy-start.12
  158.6 4.5 copy-start.7
  176.9 4.4 copy-start.5
  176.9 4.4 copy-start.6
  181.3 2.6 copy-start.24
  181.4 2.6 copy-start.25
  192.4 1.1 copy-start.1
  195.0 3.1 copy-start.4
  217.3 1.4 copy-start.2
  217.3 1.6 copy-start.3
  235.8 1.9 copy-start.8
  235.9 2.8 copy-start.11
  240.8 1.7 copy-start.9
  240.8 2.6 copy-start.12
  243.4 9.8 %copy-start.10 = (f32[2,32,24,512]{3,1,2,0:T(8,128)S(1)}, f32[2,32,24,512]{3,1,2,0:T(8,128)}, u32[]{:S(2)}) copy-start(f32[2,32,24,512]{3,1,2,0:T(8,128)} %get-tuple-element.223) | copy-start | bytes 9437188
  243.5 9.8 %copy-start.13 = (f32[2,32,24,512]{3,1,2,0:T(8,128)S(1)}, f32[2,32,24,512]{3,1,2,0:T(8,128)}, u32[]{:S(2)}) copy-start(f32[2,32,24,512]{3,1,2,0:T(8,128)} %get-tuple-element.224) | copy-start | bytes 9437188
  244.9 10.5 %collective-permute-start.4 = (f32[2,2,32,4,512]{4,2,3,1,0:T(8,128)S(1)}, f32[2,2,32,4,512]{4,2,3,1,0:T(8,128)S(1)}, u32[]{:S(2)}, u32[]{:S(2)}) collective-permute-start(f32[2,2,32,4,512]{4,2,3,1,0:T(8,128)S(1)} %fusion.46), channel_id=1, source_target_pairs={{0,1},{1,2},{2,3},{3,4},{4,5},{5,6},{6,7},{8,9},{9,10},{10,11},{11... | collective-permute-start | bytes 3145736 | tf_op jit(solution)/shard_map/ppermute | solution.py:18
  255.8 19.5 %copy-start.17 = (bf16[2,24,16,512]{3,2,1,0:T(8,128)(2,1)S(1)}, bf16[2,24,16,512]{3,2,1,0:T(8,128)(2,1)}, u32[]{:S(2)}) copy-start(bf16[2,24,16,512]{3,2,1,0:T(8,128)(2,1)} %copy-done.16) | copy-start | bytes 2359300
  255.8 19.5 %copy-start.22 = (bf16[2,24,16,512]{3,2,1,0:T(8,128)(2,1)S(1)}, bf16[2,24,16,512]{3,2,1,0:T(8,128)(2,1)}, u32[]{:S(2)}) copy-start(bf16[2,24,16,512]{3,2,1,0:T(8,128)(2,1)} %get-tuple-element.225) | copy-start | bytes 2359300
  255.8 14.8 %collective-permute-start.5 = (f32[2,2,32,4,512]{4,2,3,1,0:T(8,128)S(1)}, f32[2,2,32,4,512]{4,2,3,1,0:T(8,128)S(1)}, u32[]{:S(2)}, u32[]{:S(2)}) collective-permute-start(f32[2,2,32,4,512]{4,2,3,1,0:T(8,128)S(1)} %get-tuple-element.283), channel_id=1, source_target_pairs={{1,0},{2,1},{3,2},{4,3},{5,4},{6,5},{7,6},{9,8},{10,9},{11,10},{12... | collective-permute-start | bytes 3145736 | tf_op jit(solution)/shard_map/ppermute | solution.py:18
  271.2 9.5 %collective-permute-start.6 = (f32[2,2,4,16,512]{4,2,3,1,0:T(4,128)S(1)}, f32[2,2,4,16,512]{4,2,3,1,0:T(4,128)S(1)}, u32[]{:S(2)}, u32[]{:S(2)}) collective-permute-start(f32[2,2,4,16,512]{4,2,3,1,0:T(4,128)S(1)} %get-tuple-element.286), channel_id=1, source_target_pairs={{0,8},{8,16},{16,24},{1,9},{9,17},{17,25},{2,10},{10,18},{18,26},{... | collective-permute-start | bytes 1572872 | tf_op jit(solution)/shard_map/ppermute | solution.py:18
  274.0 11.1 %collective-permute-start.7 = (f32[2,2,4,16,512]{4,2,3,1,0:T(4,128)S(1)}, f32[2,2,4,16,512]{4,2,3,1,0:T(4,128)S(1)}, u32[]{:S(2)}, u32[]{:S(2)}) collective-permute-start(f32[2,2,4,16,512]{4,2,3,1,0:T(4,128)S(1)} %get-tuple-element.285), channel_id=1, source_target_pairs={{8,0},{16,8},{24,16},{9,1},{17,9},{25,17},{10,2},{18,10},{26,18},{... | collective-permute-start | bytes 1572872 | tf_op jit(solution)/shard_map/ppermute | solution.py:18
  277.6 8.0 %copy-start.18 = (bf16[2,24,16,512]{3,1,2,0:T(8,128)(2,1)S(1)}, bf16[2,24,16,512]{3,1,2,0:T(8,128)(2,1)}, u32[]{:S(2)}) copy-start(bf16[2,24,16,512]{3,1,2,0:T(8,128)(2,1)} %get-tuple-element.222) | copy-start | bytes 2359300
  277.6 8.0 %copy-start.21 = (bf16[2,24,16,512]{3,2,1,0:T(8,128)(2,1)S(1)}, bf16[2,24,16,512]{3,2,1,0:T(8,128)(2,1)}, u32[]{:S(2)}) copy-start(bf16[2,24,16,512]{3,2,1,0:T(8,128)(2,1)} %param.19) | copy-start | bytes 2359300
  450.2 3.4 copy-start.15
Sparse Core Ops, SparseCore 0:
  289.0 161.1 all-reduce.10
where the time goes:
time: 467 us; the launch traced here: 465 us
  waiting for transfers between devices  179 us (38%)
  local copies, waits for them, and re-layouts  162 us (35%)
  matrix products  43.7 us (9%)
  other arithmetic  37.7 us (8%)
  starting transfers between devices  25.9 us (6%)
  between operations  15.8 us (3%)
    psum x1, waiting for transfers between devices, body(): whole_qkv, whole_out = lax.psum((raw_qkv, raw_out), ('row', 'col'))  157 us
    dot_general x12, matrix products, product(): return jnp.einsum(form, left, right, preferred_element_type=jnp.float32)  35 us
    reshape x8, local copies, waits for them, and re-layouts, key_tiles(): paired.transpose(0, 2, 1, 3, 4)  27.9 us
    transpose x6, local copies, waits for them, and re-layouts, product(): return jnp.einsum(form, left, right, preferred_element_type=jnp.float32)  26.7 us
    reshape x4, local copies, waits for them, and re-layouts, fold_keys(): tile_set.reshape(tile_rows, tile_cols, 2, BLOCK, 2, BLOCK, features)  25 us
    ppermute x4, waiting for transfers between devices, passed_along(): return lax.ppermute(array, axis, pairs)  22 us
    while x54, local copies, waits for them, and re-layouts  18.2 us
    mul x9, local copies, waits for them, and re-layouts, dequantize(): mantissa.astype(jnp.float32)  17.7 us
  transfers between devices with their start and end apart: 9, of which 5 were waited for; matrix products, arithmetic and copies ran while one was open for 4% of the time, Pallas kernels for 0%

commit v1 on v0

--- a/solution.py
+++ b/solution.py
@@ -242,7 +242,7 @@
         (((0,), (0,)), ((), ())),
         preferred_element_type=jnp.float32,
     )
-    whole_qkv, whole_out = lax.psum((raw_qkv, raw_out), ("row", "col"))
+    whole_qkv, whole_out = lax.psum(lax.psum((raw_qkv, raw_out), "col"), "row")
     squares = jnp.sum(whole_qkv * whole_qkv) + jnp.sum(whole_out * whole_out)
     rows_each = features // lax.axis_size("row")
     qkv_cols = 3 * features // lax.axis_size("col")

time: 467 us -> 563 us (1.21)
  waiting for transfers between devices: 179 us -> 275 us
    psum x1 -> x2, waiting for transfers between devices: 157 us -> 253 us  [body(): whole_qkv, whole_out = lax.psum(lax.psum((raw_qkv, raw_out), 'col'), 'row')]
  transfers between devices with their start and end apart: 9 -> 10, of which waited for: 5 -> 6; matrix products, arithmetic and copies ran while one was open for 4% -> 3% of each run, Pallas kernels for 0% -> 0%
where the time goes in v1:
time: 563 us; the launch traced here: 561 us
  waiting for transfers between devices  275 us (49%)
  local copies, waits for them, and re-layouts  162 us (29%)
  matrix products  43.6 us (8%)
  other arithmetic  37.7 us (7%)
  starting transfers between devices  25.9 us (5%)
  between operations  15.8 us (3%)
    psum x2, waiting for transfers between devices, body(): whole_qkv, whole_out = lax.psum(lax.psum((raw_qkv, raw_out), 'col'), 'row')  253 us
    dot_general x12, matrix products, product(): return jnp.einsum(form, left, right, preferred_element_type=jnp.float32)  34.9 us
    reshape x8, local copies, waits for them, and re-layouts, key_tiles(): paired.transpose(0, 2, 1, 3, 4)  28 us
    transpose x6, local copies, waits for them, and re-layouts, product(): return jnp.einsum(form, left, right, preferred_element_type=jnp.float32)  26.7 us
    reshape x4, local copies, waits for them, and re-layouts, fold_keys(): tile_set.reshape(tile_rows, tile_cols, 2, BLOCK, 2, BLOCK, features)  25 us
    ppermute x4, waiting for transfers between devices, passed_along(): return lax.ppermute(array, axis, pairs)  22 us
    while x54, local copies, waits for them, and re-layouts  18.2 us
    mul x9, local copies, waits for them, and re-layouts, dequantize(): mantissa.astype(jnp.float32)  17.7 us
  transfers between devices with their start and end apart: 10, of which 6 were waited for; matrix products, arithmetic and copies ran while one was open for 3% of the time, Pallas kernels for 0%

profile of v1, /device:TPU:0, one launch (start us, length us, event | category | flops | bytes accessed | tf_op | source)
XLA Modules:
  0.0 560.7 jit_solution(5201107886812805060)
XLA Ops:
  8.2 2.1 mul.120
  10.3 3.8 mul.121
  14.1 2.1 mul.124
  16.3 3.7 mul.125
  20.0 2.9 fusion.51
  25.1 6.3 %collective-permute-start = (bf16[2,2,4,16,512]{4,3,2,1,0:T(8,128)(2,1)}, bf16[2,2,4,16,512]{4,3,2,1,0:T(8,128)(2,1)}, u32[]{:S(2)}, u32[]{:S(2)}) collective-permute-start(bf16[2,2,4,16,512]{4,3,2,1,0:T(8,128)(2,1)} %get-tuple-element.295), channel_id=1, source_target_pairs={{0,8},{8,16},{16,24},{1,9},{9,17},{17,25},{2,10},{10,18},{18,26},{... | collective-permute-start | bytes 786440 | tf_op jit(solution)/shard_map/ppermute | solution.py:29
  31.5 2.1 mul.130
  33.6 3.8 mul.131
  42.2 3.1 collective-permute-start.2
  48.0 3.2 pad_maximum_fusion.4
  51.2 1.9 slice_bitcast_fusion.8
  53.1 190.3 %while.24 = (s32[]{:T(128)}, bf16[2,24,16,512]{3,2,1,0:T(8,128)(2,1)}, bf16[2,24,16,512]{3,1,2,0:T(8,128)(2,1)}, f32[2,32,24,512]{3,1,2,0:T(8,128)}, f32[2,32,24...) while((s32[]{:T(128)}, ...), condition=%wide.region_3.4_spmd.clone, body=%wide.region_0.3_spmd.sunk.clone | while | flops 621461056 | bytes 255329296 | solution.py:219
  56.8 1.7 copy.192
  60.5 3.0 reshape.547
  63.5 4.5 copy.194
  68.8 3.0 reshape.548
  71.8 3.4 copy.196
  77.6 3.3 fusion.117
  81.8 4.4 fusion.120
  86.3 2.5 multiply_reduce_fusion.5
  88.8 2.4 copy.197
  91.2 1.7 reshape.550
  93.8 3.5 multiply_convert_fusion.6
  103.0 4.4 convolution_bitcast_fusion.12
  107.4 5.9 %copy.201 = f32[3,2,256,8,64]{4,3,2,1,0:T(8,128)} copy(f32[3,2,256,8,64]{2,4,3,1,0:T(8,128)} %convolution_bitcast_fusion.12) | data formatting | bytes 6291456 | tf_op jit(solution)/shard_map/while/body/eval_jaxpr/ijhqk,ijqhd->ijkhd/transpose | solution.py:39
  113.3 6.3 %reshape.552 = f32[3,2,2,8,2,8,512]{6,5,4,3,2,1,0:T(8,128)} reshape(f32[3,2,256,8,64]{4,3,2,1,0:T(8,128)} %copy.201) | data formatting | bytes 6291456 | tf_op jit(solution)/shard_map/while/body/eval_jaxpr/reshape | solution.py:90
  119.6 2.2 slice_bitcast_fusion.20
  123.7 2.3 convolution_bitcast_fusion.13
  126.0 5.9 %copy.203 = f32[3,2,256,8,64]{4,3,2,1,0:T(8,128)} copy(f32[3,2,256,8,64]{2,4,3,1,0:T(8,128)} %convolution_bitcast_fusion.13) | data formatting | bytes 6291456 | tf_op jit(solution)/shard_map/while/body/eval_jaxpr/ijhqk,ijqhd->ijkhd/transpose | solution.py:39
  131.8 6.3 %reshape.553 = f32[3,2,2,8,2,8,512]{6,5,4,3,2,1,0:T(8,128)} reshape(f32[3,2,256,8,64]{4,3,2,1,0:T(8,128)} %copy.203) | data formatting | bytes 6291456 | tf_op jit(solution)/shard_map/while/body/eval_jaxpr/reshape | solution.py:90
  138.1 2.2 slice_bitcast_fusion.21
  143.5 2.1 copy_dynamic-update-slice_fusion.8
  145.7 1.7 copy-done.9
  151.9 1.7 copy.192
  155.6 3.0 reshape.547
  158.6 4.5 copy.194
  163.9 3.0 reshape.548
  167.0 3.4 copy.196
  172.7 3.3 fusion.117
  177.0 4.4 fusion.120
  181.4 2.5 multiply_reduce_fusion.5
  183.9 2.4 copy.197
  186.4 1.7 reshape.550
  188.9 3.5 multiply_convert_fusion.6
  198.2 4.4 convolution_bitcast_fusion.12
  202.6 5.9 %copy.201 = f32[3,2,256,8,64]{4,3,2,1,0:T(8,128)} copy(f32[3,2,256,8,64]{2,4,3,1,0:T(8,128)} %convolution_bitcast_fusion.12) | data formatting | bytes 6291456 | tf_op jit(solution)/shard_map/while/body/eval_jaxpr/ijhqk,ijqhd->ijkhd/transpose | solution.py:39
  208.5 6.3 %reshape.552 = f32[3,2,2,8,2,8,512]{6,5,4,3,2,1,0:T(8,128)} reshape(f32[3,2,256,8,64]{4,3,2,1,0:T(8,128)} %copy.201) | data formatting | bytes 6291456 | tf_op jit(solution)/shard_map/while/body/eval_jaxpr/reshape | solution.py:90
  214.7 2.2 slice_bitcast_fusion.20
  218.9 2.3 convolution_bitcast_fusion.13
  221.2 5.9 %copy.203 = f32[3,2,256,8,64]{4,3,2,1,0:T(8,128)} copy(f32[3,2,256,8,64]{2,4,3,1,0:T(8,128)} %convolution_bitcast_fusion.13) | data formatting | bytes 6291456 | tf_op jit(solution)/shard_map/while/body/eval_jaxpr/ijhqk,ijqhd->ijkhd/transpose | solution.py:39
  227.0 6.3 %reshape.553 = f32[3,2,2,8,2,8,512]{6,5,4,3,2,1,0:T(8,128)} reshape(f32[3,2,256,8,64]{4,3,2,1,0:T(8,128)} %copy.203) | data formatting | bytes 6291456 | tf_op jit(solution)/shard_map/while/body/eval_jaxpr/reshape | solution.py:90
  233.3 2.2 slice_bitcast_fusion.21
  238.7 2.1 copy_dynamic-update-slice_fusion.8
  240.8 1.7 copy-done.9
  244.9 8.3 %collective-permute-start.4 = (f32[2,2,32,4,512]{4,2,3,1,0:T(8,128)S(1)}, f32[2,2,32,4,512]{4,2,3,1,0:T(8,128)S(1)}, u32[]{:S(2)}, u32[]{:S(2)}) collective-permute-start(f32[2,2,32,4,512]{4,2,3,1,0:T(8,128)S(1)} %fusion.46), channel_id=1, source_target_pairs={{0,1},{1,2},{2,3},{3,4},{4,5},{5,6},{6,7},{8,9},{9,10},{10,11},{11... | collective-permute-start | bytes 3145736 | tf_op jit(solution)/shard_map/ppermute | solution.py:18
  257.2 13.4 %collective-permute-done.5 = f32[2,2,32,4,512]{4,2,3,1,0:T(8,128)S(1)} collective-permute-done((f32[2,2,32,4,512]{4,2,3,1,0:T(8,128)S(1)}, f32[2,2,32,4,512]{4,2,3,1,0:T(8,128)S(1)}, u32[]{:S(2)}, u32[]{:S(2)}) %collective-permute-start.5) | collective-permute-done | bytes 1048608 | tf_op jit(solution)/shard_map/ppermute | solution.py:18
  271.1 2.9 collective-permute-start.6
  277.6 3.1 collective-permute-done.6
  280.9 4.1 collective-permute-done.7
  285.6 3.2 convolution_bitcast_fusion.3
  288.9 99.5 %all-reduce.13.cloned.1.call-done = (f32[512,1536]{0,1:T(8,128)}, f32[512,512]{1,0:T(8,128)}) async-done(((f32[512,1536]{0,1:T(8,128)}, f32[512,512]{1,0:T(8,128)}), (f32[512,1536]{0,1:T(8,128)}, f32[512,512]{1,0:T(8,128)})) %all-reduce.13.cloned.1.call-update) | async-done | bytes 4194320 | tf_op jit(solution)/shard_map/psum | solution.py:245
  390.3 2.3 fusion.43
  392.6 153.3 %all-reduce.15.cloned.1.call-done = (f32[512,1536]{0,1:T(8,128)}, f32[512,512]{1,0:T(8,128)}) async-done(((f32[512,1536]{0,1:T(8,128)}, f32[512,512]{1,0:T(8,128)}), (f32[512,1536]{0,1:T(8,128)}, f32[512,512]{1,0:T(8,128)})) %all-reduce.15.cloned.1.call-update) | async-done | bytes 4194320 | tf_op jit(solution)/shard_map/psum | solution.py:245
  545.9 3.4 multiply_reduce_fusion.1
  (210 shorter events, 70.4 us)
Async XLA Ops:
  7.2 383.1 %copy-start = (bf16[512,1536]{1,0:T(8,128)(2,1)S(1)}, bf16[512,1536]{1,0:T(8,128)(2,1)}, u32[]{:S(2)}) copy-start(bf16[512,1536]{1,0:T(8,128)(2,1)} %param.20) | copy-start | bytes 4718596
  7.2 381.2 %all-reduce.13.cloned.1.call-start = ((), (), s32[]{:S(2)}) async-start(), calls=%async_computation | async-start | bytes 8388608 | tf_op jit(solution)/shard_map/psum | solution.py:245
  23.8 15.5 %collective-permute-start.1 = (bf16[2,2,4,16,512]{4,3,2,1,0:T(8,128)(2,1)}, bf16[2,2,4,16,512]{4,3,2,1,0:T(8,128)(2,1)S(1)}, u32[]{:S(2)}, u32[]{:S(2)}) collective-permute-start(bf16[2,2,4,16,512]{4,3,2,1,0:T(8,128)(2,1)} %get-tuple-element.296), channel_id=1, source_target_pairs={{8,0},{16,8},{24,16},{9,1},{17,9},{25,17},{10,2},{18,10},{26,18},{... | collective-permute-start | bytes 786440 | tf_op jit(solution)/shard_map/ppermute | solution.py:31
  25.1 14.2 %collective-permute-start = (bf16[2,2,4,16,512]{4,3,2,1,0:T(8,128)(2,1)}, bf16[2,2,4,16,512]{4,3,2,1,0:T(8,128)(2,1)}, u32[]{:S(2)}, u32[]{:S(2)}) collective-permute-start(bf16[2,2,4,16,512]{4,3,2,1,0:T(8,128)(2,1)} %get-tuple-element.295), channel_id=1, source_target_pairs={{0,8},{8,16},{16,24},{1,9},{9,17},{17,25},{2,10},{10,18},{18,26},{... | collective-permute-start | bytes 786440 | tf_op jit(solution)/shard_map/ppermute | solution.py:29
  33.6 3.8 copy-start.20
  37.4 7.9 %copy-start.23 = (bf16[512,512]{1,0:T(8,128)(2,1)S(1)}, bf16[512,512]{1,0:T(8,128)(2,1)}, u32[]{:S(2)}) copy-start(bf16[512,512]{1,0:T(8,128)(2,1)} %param.21) | copy-start | bytes 1572868
  37.8 9.1 %copy-start.14 = (f32[2,24,16,512]{3,2,1,0:T(8,128)S(1)}, f32[2,24,16,512]{3,2,1,0:T(8,128)}, u32[]{:S(2)}) copy-start(f32[2,24,16,512]{3,2,1,0:T(8,128)} %mul.131) | copy-start | bytes 4718596
  37.8 9.1 %copy-start.19 = (bf16[2,24,16,512]{3,2,1,0:T(8,128)(2,1)S(1)}, bf16[2,24,16,512]{3,2,1,0:T(8,128)(2,1)}, u32[]{:S(2)}) copy-start(bf16[2,24,16,512]{3,2,1,0:T(8,128)(2,1)} %param.22) | copy-start | bytes 2359300
  39.3 8.8 %copy-start.16 = (bf16[2,24,16,512]{3,2,1,0:T(8,128)(2,1)}, bf16[2,24,16,512]{3,2,1,0:T(8,128)(2,1)S(1)}, u32[]{:S(2)}) copy-start(bf16[2,24,16,512]{3,2,1,0:T(8,128)(2,1)S(1)} %broadcast_select_fusion) | copy-start | bytes 2359300
  40.9 7.1 %collective-permute-start.3 = (bf16[2,2,32,4,512]{4,3,2,1,0:T(4,128)(2,1)S(1)}, bf16[2,2,32,4,512]{4,3,2,1,0:T(4,128)(2,1)S(1)}, u32[]{:S(2)}, u32[]{:S(2)}) collective-permute-start(bf16[2,2,32,4,512]{4,3,2,1,0:T(4,128)(2,1)S(1)} %get-tuple-element.294), channel_id=1, source_target_pairs={{1,0},{2,1},{3,2},{4,3},{5,4},{6,5},{7,6},{9,8},{10,9},{11,10},{12... | collective-permute-start | bytes 1572872 | tf_op jit(solution)/shard_map/ppermute | solution.py:31
  42.2 5.8 %collective-permute-start.2 = (bf16[2,2,32,4,512]{4,3,2,1,0:T(4,128)(2,1)S(1)}, bf16[2,2,32,4,512]{4,3,2,1,0:T(4,128)(2,1)S(1)}, u32[]{:S(2)}, u32[]{:S(2)}) collective-permute-start(bf16[2,2,32,4,512]{4,3,2,1,0:T(4,128)(2,1)S(1)} %get-tuple-element.293), channel_id=1, source_target_pairs={{0,1},{1,2},{2,3},{3,4},{4,5},{5,6},{6,7},{8,9},{9,10},{10,11},{11... | collective-permute-start | bytes 1572872 | tf_op jit(solution)/shard_map/ppermute | solution.py:29
  63.5 4.5 copy-start.7
  81.8 4.4 copy-start.5
  81.8 4.4 copy-start.6
  86.2 2.6 copy-start.24
  86.2 2.6 copy-start.25
  97.3 1.2 copy-start.1
  99.9 3.1 copy-start.4
  122.1 1.4 copy-start.2
  122.1 1.6 copy-start.3
  140.7 1.9 copy-start.8
  140.7 2.8 copy-start.11
  145.7 1.7 copy-start.9
  145.7 2.6 copy-start.12
  158.6 4.5 copy-start.7
  177.0 4.4 copy-start.5
  177.0 4.4 copy-start.6
  181.4 2.6 copy-start.24
  181.4 2.6 copy-start.25
  192.4 1.2 copy-start.1
  195.0 3.1 copy-start.4
  217.3 1.4 copy-start.2
  217.3 1.6 copy-start.3
  235.8 1.9 copy-start.8
  235.9 2.8 copy-start.11
  240.8 1.7 copy-start.9
  240.8 2.6 copy-start.12
  243.4 9.8 %copy-start.10 = (f32[2,32,24,512]{3,1,2,0:T(8,128)S(1)}, f32[2,32,24,512]{3,1,2,0:T(8,128)}, u32[]{:S(2)}) copy-start(f32[2,32,24,512]{3,1,2,0:T(8,128)} %get-tuple-element.223) | copy-start | bytes 9437188
  243.4 9.8 %copy-start.13 = (f32[2,32,24,512]{3,1,2,0:T(8,128)S(1)}, f32[2,32,24,512]{3,1,2,0:T(8,128)}, u32[]{:S(2)}) copy-start(f32[2,32,24,512]{3,1,2,0:T(8,128)} %get-tuple-element.224) | copy-start | bytes 9437188
  244.9 10.5 %collective-permute-start.4 = (f32[2,2,32,4,512]{4,2,3,1,0:T(8,128)S(1)}, f32[2,2,32,4,512]{4,2,3,1,0:T(8,128)S(1)}, u32[]{:S(2)}, u32[]{:S(2)}) collective-permute-start(f32[2,2,32,4,512]{4,2,3,1,0:T(8,128)S(1)} %fusion.46), channel_id=1, source_target_pairs={{0,1},{1,2},{2,3},{3,4},{4,5},{5,6},{6,7},{8,9},{9,10},{10,11},{11... | collective-permute-start | bytes 3145736 | tf_op jit(solution)/shard_map/ppermute | solution.py:18
  255.8 19.5 %copy-start.17 = (bf16[2,24,16,512]{3,2,1,0:T(8,128)(2,1)S(1)}, bf16[2,24,16,512]{3,2,1,0:T(8,128)(2,1)}, u32[]{:S(2)}) copy-start(bf16[2,24,16,512]{3,2,1,0:T(8,128)(2,1)} %copy-done.16) | copy-start | bytes 2359300
  255.8 19.5 %copy-start.22 = (bf16[2,24,16,512]{3,2,1,0:T(8,128)(2,1)S(1)}, bf16[2,24,16,512]{3,2,1,0:T(8,128)(2,1)}, u32[]{:S(2)}) copy-start(bf16[2,24,16,512]{3,2,1,0:T(8,128)(2,1)} %get-tuple-element.225) | copy-start | bytes 2359300
  255.8 14.8 %collective-permute-start.5 = (f32[2,2,32,4,512]{4,2,3,1,0:T(8,128)S(1)}, f32[2,2,32,4,512]{4,2,3,1,0:T(8,128)S(1)}, u32[]{:S(2)}, u32[]{:S(2)}) collective-permute-start(f32[2,2,32,4,512]{4,2,3,1,0:T(8,128)S(1)} %get-tuple-element.285), channel_id=1, source_target_pairs={{1,0},{2,1},{3,2},{4,3},{5,4},{6,5},{7,6},{9,8},{10,9},{11,10},{12... | collective-permute-start | bytes 3145736 | tf_op jit(solution)/shard_map/ppermute | solution.py:18
  271.1 9.5 %collective-permute-start.6 = (f32[2,2,4,16,512]{4,2,3,1,0:T(4,128)S(1)}, f32[2,2,4,16,512]{4,2,3,1,0:T(4,128)S(1)}, u32[]{:S(2)}, u32[]{:S(2)}) collective-permute-start(f32[2,2,4,16,512]{4,2,3,1,0:T(4,128)S(1)} %get-tuple-element.288), channel_id=1, source_target_pairs={{0,8},{8,16},{16,24},{1,9},{9,17},{17,25},{2,10},{10,18},{18,26},{... | collective-permute-start | bytes 1572872 | tf_op jit(solution)/shard_map/ppermute | solution.py:18
  274.0 11.1 %collective-permute-start.7 = (f32[2,2,4,16,512]{4,2,3,1,0:T(4,128)S(1)}, f32[2,2,4,16,512]{4,2,3,1,0:T(4,128)S(1)}, u32[]{:S(2)}, u32[]{:S(2)}) collective-permute-start(f32[2,2,4,16,512]{4,2,3,1,0:T(4,128)S(1)} %get-tuple-element.287), channel_id=1, source_target_pairs={{8,0},{16,8},{24,16},{9,1},{17,9},{25,17},{10,2},{18,10},{26,18},{... | collective-permute-start | bytes 1572872 | tf_op jit(solution)/shard_map/ppermute | solution.py:18
  277.5 8.0 %copy-start.18 = (bf16[2,24,16,512]{3,1,2,0:T(8,128)(2,1)S(1)}, bf16[2,24,16,512]{3,1,2,0:T(8,128)(2,1)}, u32[]{:S(2)}) copy-start(bf16[2,24,16,512]{3,1,2,0:T(8,128)(2,1)} %get-tuple-element.222) | copy-start | bytes 2359300
  277.5 8.0 %copy-start.21 = (bf16[2,24,16,512]{3,2,1,0:T(8,128)(2,1)S(1)}, bf16[2,24,16,512]{3,2,1,0:T(8,128)(2,1)}, u32[]{:S(2)}) copy-start(bf16[2,24,16,512]{3,2,1,0:T(8,128)(2,1)} %param.19) | copy-start | bytes 2359300
  288.8 257.0 %all-reduce.15.cloned.1.call-start = ((), (), s32[]{:S(2)}) async-start(), calls=%async_computation.1 | async-start | bytes 8388608 | tf_op jit(solution)/shard_map/psum | solution.py:245
  545.9 3.4 copy-start.15
Sparse Core Ops, SparseCore 0:
  289.0 99.3 all-reduce.12
  390.8 155.0 all-reduce.14
